TPU v7x, 256 devices: a whole 4x4x8 slice. The times are simulated.
256 devices in a mesh: req: 16 (over x, y), seq: 16 (over z, core).
Axes of the slice: x: 4, y: 4, z: 8, core: 2. Of those that a mesh axis runs over, the one named last changes fastest.
Arguments:
- store: bfloat16 [144, 16, 56, 1024], P('req', 'seq'), may hold values from -6 to 6
- passage_owner: int32 [16, 256, 1], P(None, 'seq'), may hold values from 0 to 15; in each aligned block of 16 rows (0 to 15, 16 to 31, ..., all dimensions but the last counted through in order) at most 2 rows name the same one
- passage_slot: int32 [16, 256], P(None, 'seq'), may hold values from 0 to 8
- sel_pos: int32 [16, 1792], P('req'), may hold values from 0 to 14335, as said below
- queries: bfloat16 [16, 1792, 2048], P('req', 'seq'), may hold values from -512 to 512
- new_kv: bfloat16 [16, 1792, 1024], P('req', 'seq'), may hold values from -6 to 6
Outputs:
- blended_kv: bfloat16 [16, 14336, 1024], P('req', 'seq')
- deviation: float32 [16, 1792, 4], P('req', 'seq')
- attended: bfloat16 [16, 1792, 2048], P('req', 'seq')
Inputs may be any that keep to these rules, and one draw needn't show every extreme that they name: `passage_owner`: within the 16 pieces of one request's position block no owner is named more than 2 times, and some block names one owner exactly 2 times. `sel_pos`: entries b * 112 to (b + 1) * 112 - 1 of a request are distinct positions of block b, between b * 896 and (b + 1) * 896 - 1.
All inputs are finite; a program needn't handle non-finite values.
Results may differ from a plain program's by a relative error of at most 0.005.
Values may be sent and summed in bfloat16 or wider, within the bound.
A program may use at most 128 MiB of HBM per device.

v0:
```python
import jax
import jax.numpy as jnp
from jax import lax
from jax.sharding import PartitionSpec as P

HEAD_DIM = 128
KV_HEADS = 4
PASSAGE = 56
PASSAGES_DEV = 16
TOK_DEV = 896
SEL_DEV = 112
Q_WIDTH = 2048
KV_WIDTH = 1024
GROUP = 4


def update(carry_state, query_rows, query_pos, key_rows, value_rows, key_pos):
    running_max, weight_sum, summed = carry_state
    row_count = query_rows.shape[0]
    score_scale = HEAD_DIM ** (-0.5)
    query_split = query_rows.reshape(row_count, KV_HEADS, GROUP, HEAD_DIM)
    scores = (
        jnp.einsum("qkgd,pkd->qkgp", query_split, key_rows, preferred_element_type=jnp.float32)
        * score_scale
    )
    visible = key_pos[None, None, None, :] <= query_pos[:, None, None, None]
    scores = jnp.where(visible, scores, -1e30)
    new_max = jnp.maximum(running_max, jnp.max(scores, axis=-1))
    weights = jnp.where(visible, jnp.exp(scores - new_max[..., None]), 0.0)
    rescale = jnp.exp(running_max - new_max)
    weight_sum = weight_sum * rescale + jnp.sum(weights, axis=-1)
    product = jnp.einsum(
        "qkgp,pkd->qkgd",
        weights.astype(jnp.bfloat16),
        value_rows,
        preferred_element_type=jnp.float32,
    )
    summed = summed * rescale[..., None] + product
    return (new_max, weight_sum, summed)


def fold_attention(groups, blended):
    initial = []
    for query_rows, query_pos in groups:
        row_count = query_rows.shape[0]
        initial.append(
            (
                jnp.full((row_count, KV_HEADS, GROUP), -1e30, jnp.float32),
                jnp.zeros((row_count, KV_HEADS, GROUP), jnp.float32),
                jnp.zeros((row_count, KV_HEADS, GROUP, HEAD_DIM), jnp.float32),
            )
        )
    carry_all = tuple(initial)
    piece = lax.all_gather(blended, "seq", axis=0, tiled=True)
    absorb_row_count = piece.shape[0]
    block_rows = 512

    def take_block(state_all, step_index):
        key_part = lax.dynamic_slice_in_dim(piece, step_index * block_rows, block_rows, 0)
        first_pos = step_index * block_rows
        key_rows = key_part[:, : KV_HEADS * HEAD_DIM].reshape(block_rows, KV_HEADS, HEAD_DIM)
        value_rows = key_part[:, KV_HEADS * HEAD_DIM :].reshape(block_rows, KV_HEADS, HEAD_DIM)
        key_pos = first_pos + jnp.arange(block_rows, dtype=jnp.int32)
        updated = []
        for (query_rows, query_pos), carry_state in zip(groups, state_all):
            updated.append(
                lax.cond(
                    first_pos <= jnp.max(query_pos),
                    lambda state_in: update(
                        state_in, query_rows, query_pos, key_rows, value_rows, key_pos
                    ),
                    lambda state_in: state_in,
                    carry_state,
                )
            )
        return (tuple(updated), None)

    carry_all, _ = lax.scan(take_block, carry_all, jnp.arange(absorb_row_count // block_rows))
    finished = []
    for (query_rows, query_pos), carry_state in zip(groups, carry_all):
        row_count = query_rows.shape[0]
        output_rows = carry_state[2] / carry_state[1][..., None]
        finished.append(output_rows.reshape(row_count, Q_WIDTH).astype(jnp.bfloat16))
    return finished


def body(store, passage_owner, passage_slot, sel_pos, queries, new_kv):
    req_index = lax.axis_index("req")
    seq_index = lax.axis_index("seq")
    owner_table = passage_owner[:, :, 0]
    my_owner = lax.dynamic_index_in_dim(owner_table, req_index, 0, keepdims=False)
    store_shard = store[:, 0]
    req_count = owner_table.shape[0]
    owner_cap = max(2, (2 * PASSAGES_DEV + req_count - 1) // req_count)
    earlier = jnp.arange(PASSAGES_DEV)[:, None] > jnp.arange(PASSAGES_DEV)[None, :]
    same_owner = owner_table[:, :, None] == owner_table[:, None, :]
    rank_table = jnp.sum(same_owner & earlier[None], axis=2)
    slot_hit = (owner_table == req_index)[:, :, None] & (
        rank_table[:, :, None] == jnp.arange(owner_cap)[None, None, :]
    )
    send_slot = jnp.sum(jnp.where(slot_hit, passage_slot[:, :, None], 0), axis=1)
    outgoing = jnp.take(store_shard, send_slot.reshape(-1), axis=0)
    outgoing = outgoing.reshape(req_count, owner_cap, PASSAGE, KV_WIDTH)
    incoming = lax.all_to_all(outgoing, "req", split_axis=0, concat_axis=0, tiled=True)
    my_rank = lax.dynamic_index_in_dim(rank_table, req_index, 0, keepdims=False)
    flat_slot = my_owner * owner_cap + my_rank
    cached = jnp.take(incoming.reshape(req_count * owner_cap, PASSAGE, KV_WIDTH), flat_slot, axis=0)
    cached = cached.reshape(TOK_DEV, KV_WIDTH)
    all_pos = sel_pos[0]
    own_pos = lax.dynamic_slice_in_dim(all_pos, seq_index * SEL_DEV, SEL_DEV)
    offset = own_pos - seq_index * TOK_DEV
    fresh_rows = new_kv[0]
    picked = jnp.take(cached, offset, axis=0)
    blended = cached.at[offset].set(fresh_rows)
    difference = fresh_rows.astype(jnp.float32) - picked.astype(jnp.float32)
    squared = (difference * difference).reshape(SEL_DEV, 2, KV_HEADS, HEAD_DIM)
    deviation = jnp.sum(squared, axis=(1, 3))
    query_local = queries[0]
    attended = fold_attention([(query_local, own_pos)], blended)[0]
    return (blended[None], deviation[None], attended[None])


def solution(mesh):
    placed = (
        P("req", "seq", None, None),
        P(None, "seq", None),
        P(None, "seq"),
        P("req", None),
        P("req", "seq", None),
        P("req", "seq", None),
    )
    return jax.shard_map(
        body,
        mesh=mesh,
        in_specs=placed,
        out_specs=(P("req", "seq", None), P("req", "seq", None), P("req", "seq", None)),
        check_vma=False,
    )
```

profile of v0, /device:TPU:225, one launch (start us, length us, event | category | flops | bytes accessed | tf_op | source)
XLA Modules:
  0.0 505.5 jit_solution(7057776193855823319)
XLA Ops:
  10.3 2.6 gather_fusion
  13.0 4.2 broadcast_select_fusion
  17.2 6.8 %all-to-all-start = ((bf16[16,2,56,1024]{3,2,1,0:T(8,128)(2,1)}), bf16[16,2,56,1024]{3,2,1,0:T(8,128)(2,1)}, u32[]{:S(2)}, u32[]{:S(2)}) async-start(bf16[16,2,56,1024]{3,2,1,0:T(8,128)(2,1)} %broadcast_select_fusion), calls=%async_computation | async-start | bytes 7340032 | tf_op jit(solution)/shard_map/all_to_all | solution.py:104
  27.0 45.7 %all-to-all-done = bf16[16,2,56,1024]{3,2,1,0:T(8,128)(2,1)} async-done(((bf16[16,2,56,1024]{3,2,1,0:T(8,128)(2,1)}), bf16[16,2,56,1024]{3,2,1,0:T(8,128)(2,1)}, u32[]{:S(2)}, u32[]{:S(2)}) %all-to-all-start) | async-done | bytes 3670048 | tf_op jit(solution)/shard_map/all_to_all | solution.py:104
  72.7 3.9 gather_fusion.1
  79.3 2.1 scatter_custom_fusion
  84.1 158.5 %all-gather.2.cloned.1.call-done = bf16[14336,1024]{1,0:T(8,128)(2,1)} async-done(((bf16[896,1024]{1,0:T(8,128)(2,1)}), bf16[14336,1024]{1,0:T(8,128)(2,1)}) %all-gather.2.cloned.1.call-update) | async-done | bytes 29360144 | tf_op jit(solution)/shard_map/all_gather | solution.py:54
  242.6 35.1 %copy.27 = bf16[14336,1024]{0,1:T(8,128)(2,1)} copy(bf16[14336,1024]{1,0:T(8,128)(2,1)} %all-gather.2.cloned.1.call-done) | data formatting | bytes 58720256 | tf_op jit(solution)/shard_map/while | solution.py:78
  277.8 219.3 %while.15 = (s32[]{:T(128)}, f32[112,4,4]{0,2,1:T(4,128)S(1)}, f32[112,4,4]{0,2,1:T(4,128)S(1)}, f32[112,4,4,128]{3,0,2,1:T(8,128)S(1)}, s32[28]{0:T(128)S(1)}, ...) while((s32[]{:T(128)}, f32[112,4,4]{0,2,1:T(4,128)S(1)}, ...), condition=%wide.region_10.11_spmd, body=%wide.region_5.10_spmd.sunk | while | flops 482209792 | bytes 17720068 | solution.py:78
  279.7 5.9 %conditional.2 = ((f32[112,4,4]{0,2,1:T(4,128)S(1)}, f32[112,4,4]{0,2,1:T(4,128)S(1)}, f32[112,4,4,128]{3,0,2,1:T(8,128)S(1)})) conditional(s32[]{:T(128)} %convert_element_type.61, (f32[112,4,4]{0,2,1:T(4,128)S(1)}, f32[112,4,4]{0,2,1:T(4,128)S(1)}, f32[112,4,4,128]{3,0,2,1:T(8,128)S(1)}) %tuple.51, (s32[]{:T(128)}, s32[512]{0:T(512)S(1)}, ...), branch_computations={%region_6.6_spmd, %region_7.9_spmd} | conditional | flops 482209792 | bytes 17717786 | solution.py:67
  287.5 5.9 %conditional.2 = ((f32[112,4,4]{0,2,1:T(4,128)S(1)}, f32[112,4,4]{0,2,1:T(4,128)S(1)}, f32[112,4,4,128]{3,0,2,1:T(8,128)S(1)})) conditional(s32[]{:T(128)} %convert_element_type.61, (f32[112,4,4]{0,2,1:T(4,128)S(1)}, f32[112,4,4]{0,2,1:T(4,128)S(1)}, f32[112,4,4,128]{3,0,2,1:T(8,128)S(1)}) %tuple.51, (s32[]{:T(128)}, s32[512]{0:T(512)S(1)}, ...), branch_computations={%region_6.6_spmd, %region_7.9_spmd} | conditional | flops 482209792 | bytes 17717786 | solution.py:67
  287.5 1.9 fusion.25
  295.4 5.9 %conditional.2 = ((f32[112,4,4]{0,2,1:T(4,128)S(1)}, f32[112,4,4]{0,2,1:T(4,128)S(1)}, f32[112,4,4,128]{3,0,2,1:T(8,128)S(1)})) conditional(s32[]{:T(128)} %convert_element_type.61, (f32[112,4,4]{0,2,1:T(4,128)S(1)}, f32[112,4,4]{0,2,1:T(4,128)S(1)}, f32[112,4,4,128]{3,0,2,1:T(8,128)S(1)}) %tuple.51, (s32[]{:T(128)}, s32[512]{0:T(512)S(1)}, ...), branch_computations={%region_6.6_spmd, %region_7.9_spmd} | conditional | flops 482209792 | bytes 17717786 | solution.py:67
  303.2 5.9 %conditional.2 = ((f32[112,4,4]{0,2,1:T(4,128)S(1)}, f32[112,4,4]{0,2,1:T(4,128)S(1)}, f32[112,4,4,128]{3,0,2,1:T(8,128)S(1)})) conditional(s32[]{:T(128)} %convert_element_type.61, (f32[112,4,4]{0,2,1:T(4,128)S(1)}, f32[112,4,4]{0,2,1:T(4,128)S(1)}, f32[112,4,4,128]{3,0,2,1:T(8,128)S(1)}) %tuple.51, (s32[]{:T(128)}, s32[512]{0:T(512)S(1)}, ...), branch_computations={%region_6.6_spmd, %region_7.9_spmd} | conditional | flops 482209792 | bytes 17717786 | solution.py:67
  303.2 1.9 fusion.25
  311.0 5.9 %conditional.2 = ((f32[112,4,4]{0,2,1:T(4,128)S(1)}, f32[112,4,4]{0,2,1:T(4,128)S(1)}, f32[112,4,4,128]{3,0,2,1:T(8,128)S(1)})) conditional(s32[]{:T(128)} %convert_element_type.61, (f32[112,4,4]{0,2,1:T(4,128)S(1)}, f32[112,4,4]{0,2,1:T(4,128)S(1)}, f32[112,4,4,128]{3,0,2,1:T(8,128)S(1)}) %tuple.51, (s32[]{:T(128)}, s32[512]{0:T(512)S(1)}, ...), branch_computations={%region_6.6_spmd, %region_7.9_spmd} | conditional | flops 482209792 | bytes 17717786 | solution.py:67
  311.0 1.9 fusion.25
  318.9 5.9 %conditional.2 = ((f32[112,4,4]{0,2,1:T(4,128)S(1)}, f32[112,4,4]{0,2,1:T(4,128)S(1)}, f32[112,4,4,128]{3,0,2,1:T(8,128)S(1)})) conditional(s32[]{:T(128)} %convert_element_type.61, (f32[112,4,4]{0,2,1:T(4,128)S(1)}, f32[112,4,4]{0,2,1:T(4,128)S(1)}, f32[112,4,4,128]{3,0,2,1:T(8,128)S(1)}) %tuple.51, (s32[]{:T(128)}, s32[512]{0:T(512)S(1)}, ...), branch_computations={%region_6.6_spmd, %region_7.9_spmd} | conditional | flops 482209792 | bytes 17717786 | solution.py:67
  318.9 1.9 fusion.25
  326.7 5.9 %conditional.2 = ((f32[112,4,4]{0,2,1:T(4,128)S(1)}, f32[112,4,4]{0,2,1:T(4,128)S(1)}, f32[112,4,4,128]{3,0,2,1:T(8,128)S(1)})) conditional(s32[]{:T(128)} %convert_element_type.61, (f32[112,4,4]{0,2,1:T(4,128)S(1)}, f32[112,4,4]{0,2,1:T(4,128)S(1)}, f32[112,4,4,128]{3,0,2,1:T(8,128)S(1)}) %tuple.51, (s32[]{:T(128)}, s32[512]{0:T(512)S(1)}, ...), branch_computations={%region_6.6_spmd, %region_7.9_spmd} | conditional | flops 482209792 | bytes 17717786 | solution.py:67
  326.7 1.9 fusion.25
  334.5 5.9 %conditional.2 = ((f32[112,4,4]{0,2,1:T(4,128)S(1)}, f32[112,4,4]{0,2,1:T(4,128)S(1)}, f32[112,4,4,128]{3,0,2,1:T(8,128)S(1)})) conditional(s32[]{:T(128)} %convert_element_type.61, (f32[112,4,4]{0,2,1:T(4,128)S(1)}, f32[112,4,4]{0,2,1:T(4,128)S(1)}, f32[112,4,4,128]{3,0,2,1:T(8,128)S(1)}) %tuple.51, (s32[]{:T(128)}, s32[512]{0:T(512)S(1)}, ...), branch_computations={%region_6.6_spmd, %region_7.9_spmd} | conditional | flops 482209792 | bytes 17717786 | solution.py:67
  334.6 1.9 fusion.25
  342.4 5.9 %conditional.2 = ((f32[112,4,4]{0,2,1:T(4,128)S(1)}, f32[112,4,4]{0,2,1:T(4,128)S(1)}, f32[112,4,4,128]{3,0,2,1:T(8,128)S(1)})) conditional(s32[]{:T(128)} %convert_element_type.61, (f32[112,4,4]{0,2,1:T(4,128)S(1)}, f32[112,4,4]{0,2,1:T(4,128)S(1)}, f32[112,4,4,128]{3,0,2,1:T(8,128)S(1)}) %tuple.51, (s32[]{:T(128)}, s32[512]{0:T(512)S(1)}, ...), branch_computations={%region_6.6_spmd, %region_7.9_spmd} | conditional | flops 482209792 | bytes 17717786 | solution.py:67
  342.4 1.9 fusion.25
  350.2 5.9 %conditional.2 = ((f32[112,4,4]{0,2,1:T(4,128)S(1)}, f32[112,4,4]{0,2,1:T(4,128)S(1)}, f32[112,4,4,128]{3,0,2,1:T(8,128)S(1)})) conditional(s32[]{:T(128)} %convert_element_type.61, (f32[112,4,4]{0,2,1:T(4,128)S(1)}, f32[112,4,4]{0,2,1:T(4,128)S(1)}, f32[112,4,4,128]{3,0,2,1:T(8,128)S(1)}) %tuple.51, (s32[]{:T(128)}, s32[512]{0:T(512)S(1)}, ...), branch_computations={%region_6.6_spmd, %region_7.9_spmd} | conditional | flops 482209792 | bytes 17717786 | solution.py:67
  350.2 1.9 fusion.25
  358.0 5.9 %conditional.2 = ((f32[112,4,4]{0,2,1:T(4,128)S(1)}, f32[112,4,4]{0,2,1:T(4,128)S(1)}, f32[112,4,4,128]{3,0,2,1:T(8,128)S(1)})) conditional(s32[]{:T(128)} %convert_element_type.61, (f32[112,4,4]{0,2,1:T(4,128)S(1)}, f32[112,4,4]{0,2,1:T(4,128)S(1)}, f32[112,4,4,128]{3,0,2,1:T(8,128)S(1)}) %tuple.51, (s32[]{:T(128)}, s32[512]{0:T(512)S(1)}, ...), branch_computations={%region_6.6_spmd, %region_7.9_spmd} | conditional | flops 482209792 | bytes 17717786 | solution.py:67
  358.1 1.9 fusion.25
  365.9 5.9 %conditional.2 = ((f32[112,4,4]{0,2,1:T(4,128)S(1)}, f32[112,4,4]{0,2,1:T(4,128)S(1)}, f32[112,4,4,128]{3,0,2,1:T(8,128)S(1)})) conditional(s32[]{:T(128)} %convert_element_type.61, (f32[112,4,4]{0,2,1:T(4,128)S(1)}, f32[112,4,4]{0,2,1:T(4,128)S(1)}, f32[112,4,4,128]{3,0,2,1:T(8,128)S(1)}) %tuple.51, (s32[]{:T(128)}, s32[512]{0:T(512)S(1)}, ...), branch_computations={%region_6.6_spmd, %region_7.9_spmd} | conditional | flops 482209792 | bytes 17717786 | solution.py:67
  365.9 1.9 fusion.25
  373.7 5.9 %conditional.2 = ((f32[112,4,4]{0,2,1:T(4,128)S(1)}, f32[112,4,4]{0,2,1:T(4,128)S(1)}, f32[112,4,4,128]{3,0,2,1:T(8,128)S(1)})) conditional(s32[]{:T(128)} %convert_element_type.61, (f32[112,4,4]{0,2,1:T(4,128)S(1)}, f32[112,4,4]{0,2,1:T(4,128)S(1)}, f32[112,4,4,128]{3,0,2,1:T(8,128)S(1)}) %tuple.51, (s32[]{:T(128)}, s32[512]{0:T(512)S(1)}, ...), branch_computations={%region_6.6_spmd, %region_7.9_spmd} | conditional | flops 482209792 | bytes 17717786 | solution.py:67
  373.7 1.9 fusion.25
  381.5 5.9 %conditional.2 = ((f32[112,4,4]{0,2,1:T(4,128)S(1)}, f32[112,4,4]{0,2,1:T(4,128)S(1)}, f32[112,4,4,128]{3,0,2,1:T(8,128)S(1)})) conditional(s32[]{:T(128)} %convert_element_type.61, (f32[112,4,4]{0,2,1:T(4,128)S(1)}, f32[112,4,4]{0,2,1:T(4,128)S(1)}, f32[112,4,4,128]{3,0,2,1:T(8,128)S(1)}) %tuple.51, (s32[]{:T(128)}, s32[512]{0:T(512)S(1)}, ...), branch_computations={%region_6.6_spmd, %region_7.9_spmd} | conditional | flops 482209792 | bytes 17717786 | solution.py:67
  389.4 5.9 %conditional.2 = ((f32[112,4,4]{0,2,1:T(4,128)S(1)}, f32[112,4,4]{0,2,1:T(4,128)S(1)}, f32[112,4,4,128]{3,0,2,1:T(8,128)S(1)})) conditional(s32[]{:T(128)} %convert_element_type.61, (f32[112,4,4]{0,2,1:T(4,128)S(1)}, f32[112,4,4]{0,2,1:T(4,128)S(1)}, f32[112,4,4,128]{3,0,2,1:T(8,128)S(1)}) %tuple.51, (s32[]{:T(128)}, s32[512]{0:T(512)S(1)}, ...), branch_computations={%region_6.6_spmd, %region_7.9_spmd} | conditional | flops 482209792 | bytes 17717786 | solution.py:67
  397.2 5.9 %conditional.2 = ((f32[112,4,4]{0,2,1:T(4,128)S(1)}, f32[112,4,4]{0,2,1:T(4,128)S(1)}, f32[112,4,4,128]{3,0,2,1:T(8,128)S(1)})) conditional(s32[]{:T(128)} %convert_element_type.61, (f32[112,4,4]{0,2,1:T(4,128)S(1)}, f32[112,4,4]{0,2,1:T(4,128)S(1)}, f32[112,4,4,128]{3,0,2,1:T(8,128)S(1)}) %tuple.51, (s32[]{:T(128)}, s32[512]{0:T(512)S(1)}, ...), branch_computations={%region_6.6_spmd, %region_7.9_spmd} | conditional | flops 482209792 | bytes 17717786 | solution.py:67
  405.0 5.9 %conditional.2 = ((f32[112,4,4]{0,2,1:T(4,128)S(1)}, f32[112,4,4]{0,2,1:T(4,128)S(1)}, f32[112,4,4,128]{3,0,2,1:T(8,128)S(1)})) conditional(s32[]{:T(128)} %convert_element_type.61, (f32[112,4,4]{0,2,1:T(4,128)S(1)}, f32[112,4,4]{0,2,1:T(4,128)S(1)}, f32[112,4,4,128]{3,0,2,1:T(8,128)S(1)}) %tuple.51, (s32[]{:T(128)}, s32[512]{0:T(512)S(1)}, ...), branch_computations={%region_6.6_spmd, %region_7.9_spmd} | conditional | flops 482209792 | bytes 17717786 | solution.py:67
  412.9 5.9 %conditional.2 = ((f32[112,4,4]{0,2,1:T(4,128)S(1)}, f32[112,4,4]{0,2,1:T(4,128)S(1)}, f32[112,4,4,128]{3,0,2,1:T(8,128)S(1)})) conditional(s32[]{:T(128)} %convert_element_type.61, (f32[112,4,4]{0,2,1:T(4,128)S(1)}, f32[112,4,4]{0,2,1:T(4,128)S(1)}, f32[112,4,4,128]{3,0,2,1:T(8,128)S(1)}) %tuple.51, (s32[]{:T(128)}, s32[512]{0:T(512)S(1)}, ...), branch_computations={%region_6.6_spmd, %region_7.9_spmd} | conditional | flops 482209792 | bytes 17717786 | solution.py:67
  420.7 5.9 %conditional.2 = ((f32[112,4,4]{0,2,1:T(4,128)S(1)}, f32[112,4,4]{0,2,1:T(4,128)S(1)}, f32[112,4,4,128]{3,0,2,1:T(8,128)S(1)})) conditional(s32[]{:T(128)} %convert_element_type.61, (f32[112,4,4]{0,2,1:T(4,128)S(1)}, f32[112,4,4]{0,2,1:T(4,128)S(1)}, f32[112,4,4,128]{3,0,2,1:T(8,128)S(1)}) %tuple.51, (s32[]{:T(128)}, s32[512]{0:T(512)S(1)}, ...), branch_computations={%region_6.6_spmd, %region_7.9_spmd} | conditional | flops 482209792 | bytes 17717786 | solution.py:67
  428.5 5.9 %conditional.2 = ((f32[112,4,4]{0,2,1:T(4,128)S(1)}, f32[112,4,4]{0,2,1:T(4,128)S(1)}, f32[112,4,4,128]{3,0,2,1:T(8,128)S(1)})) conditional(s32[]{:T(128)} %convert_element_type.61, (f32[112,4,4]{0,2,1:T(4,128)S(1)}, f32[112,4,4]{0,2,1:T(4,128)S(1)}, f32[112,4,4,128]{3,0,2,1:T(8,128)S(1)}) %tuple.51, (s32[]{:T(128)}, s32[512]{0:T(512)S(1)}, ...), branch_computations={%region_6.6_spmd, %region_7.9_spmd} | conditional | flops 482209792 | bytes 17717786 | solution.py:67
  436.4 5.9 %conditional.2 = ((f32[112,4,4]{0,2,1:T(4,128)S(1)}, f32[112,4,4]{0,2,1:T(4,128)S(1)}, f32[112,4,4,128]{3,0,2,1:T(8,128)S(1)})) conditional(s32[]{:T(128)} %convert_element_type.61, (f32[112,4,4]{0,2,1:T(4,128)S(1)}, f32[112,4,4]{0,2,1:T(4,128)S(1)}, f32[112,4,4,128]{3,0,2,1:T(8,128)S(1)}) %tuple.51, (s32[]{:T(128)}, s32[512]{0:T(512)S(1)}, ...), branch_computations={%region_6.6_spmd, %region_7.9_spmd} | conditional | flops 482209792 | bytes 17717786 | solution.py:67
  444.2 5.9 %conditional.2 = ((f32[112,4,4]{0,2,1:T(4,128)S(1)}, f32[112,4,4]{0,2,1:T(4,128)S(1)}, f32[112,4,4,128]{3,0,2,1:T(8,128)S(1)})) conditional(s32[]{:T(128)} %convert_element_type.61, (f32[112,4,4]{0,2,1:T(4,128)S(1)}, f32[112,4,4]{0,2,1:T(4,128)S(1)}, f32[112,4,4,128]{3,0,2,1:T(8,128)S(1)}) %tuple.51, (s32[]{:T(128)}, s32[512]{0:T(512)S(1)}, ...), branch_computations={%region_6.6_spmd, %region_7.9_spmd} | conditional | flops 482209792 | bytes 17717786 | solution.py:67
  452.0 5.9 %conditional.2 = ((f32[112,4,4]{0,2,1:T(4,128)S(1)}, f32[112,4,4]{0,2,1:T(4,128)S(1)}, f32[112,4,4,128]{3,0,2,1:T(8,128)S(1)})) conditional(s32[]{:T(128)} %convert_element_type.61, (f32[112,4,4]{0,2,1:T(4,128)S(1)}, f32[112,4,4]{0,2,1:T(4,128)S(1)}, f32[112,4,4,128]{3,0,2,1:T(8,128)S(1)}) %tuple.51, (s32[]{:T(128)}, s32[512]{0:T(512)S(1)}, ...), branch_computations={%region_6.6_spmd, %region_7.9_spmd} | conditional | flops 482209792 | bytes 17717786 | solution.py:67
  459.9 5.9 %conditional.2 = ((f32[112,4,4]{0,2,1:T(4,128)S(1)}, f32[112,4,4]{0,2,1:T(4,128)S(1)}, f32[112,4,4,128]{3,0,2,1:T(8,128)S(1)})) conditional(s32[]{:T(128)} %convert_element_type.61, (f32[112,4,4]{0,2,1:T(4,128)S(1)}, f32[112,4,4]{0,2,1:T(4,128)S(1)}, f32[112,4,4,128]{3,0,2,1:T(8,128)S(1)}) %tuple.51, (s32[]{:T(128)}, s32[512]{0:T(512)S(1)}, ...), branch_computations={%region_6.6_spmd, %region_7.9_spmd} | conditional | flops 482209792 | bytes 17717786 | solution.py:67
  467.7 5.9 %conditional.2 = ((f32[112,4,4]{0,2,1:T(4,128)S(1)}, f32[112,4,4]{0,2,1:T(4,128)S(1)}, f32[112,4,4,128]{3,0,2,1:T(8,128)S(1)})) conditional(s32[]{:T(128)} %convert_element_type.61, (f32[112,4,4]{0,2,1:T(4,128)S(1)}, f32[112,4,4]{0,2,1:T(4,128)S(1)}, f32[112,4,4,128]{3,0,2,1:T(8,128)S(1)}) %tuple.51, (s32[]{:T(128)}, s32[512]{0:T(512)S(1)}, ...), branch_computations={%region_6.6_spmd, %region_7.9_spmd} | conditional | flops 482209792 | bytes 17717786 | solution.py:67
  475.5 5.9 %conditional.2 = ((f32[112,4,4]{0,2,1:T(4,128)S(1)}, f32[112,4,4]{0,2,1:T(4,128)S(1)}, f32[112,4,4,128]{3,0,2,1:T(8,128)S(1)})) conditional(s32[]{:T(128)} %convert_element_type.61, (f32[112,4,4]{0,2,1:T(4,128)S(1)}, f32[112,4,4]{0,2,1:T(4,128)S(1)}, f32[112,4,4,128]{3,0,2,1:T(8,128)S(1)}) %tuple.51, (s32[]{:T(128)}, s32[512]{0:T(512)S(1)}, ...), branch_computations={%region_6.6_spmd, %region_7.9_spmd} | conditional | flops 482209792 | bytes 17717786 | solution.py:67
  483.4 5.9 %conditional.2 = ((f32[112,4,4]{0,2,1:T(4,128)S(1)}, f32[112,4,4]{0,2,1:T(4,128)S(1)}, f32[112,4,4,128]{3,0,2,1:T(8,128)S(1)})) conditional(s32[]{:T(128)} %convert_element_type.61, (f32[112,4,4]{0,2,1:T(4,128)S(1)}, f32[112,4,4]{0,2,1:T(4,128)S(1)}, f32[112,4,4,128]{3,0,2,1:T(8,128)S(1)}) %tuple.51, (s32[]{:T(128)}, s32[512]{0:T(512)S(1)}, ...), branch_computations={%region_6.6_spmd, %region_7.9_spmd} | conditional | flops 482209792 | bytes 17717786 | solution.py:67
  491.2 5.8 %conditional.2 = ((f32[112,4,4]{0,2,1:T(4,128)S(1)}, f32[112,4,4]{0,2,1:T(4,128)S(1)}, f32[112,4,4,128]{3,0,2,1:T(8,128)S(1)})) conditional(s32[]{:T(128)} %convert_element_type.61, (f32[112,4,4]{0,2,1:T(4,128)S(1)}, f32[112,4,4]{0,2,1:T(4,128)S(1)}, f32[112,4,4,128]{3,0,2,1:T(8,128)S(1)}) %tuple.51, (s32[]{:T(128)}, s32[512]{0:T(512)S(1)}, ...), branch_computations={%region_6.6_spmd, %region_7.9_spmd} | conditional | flops 482209792 | bytes 17717786 | solution.py:67
  (370 shorter events, 173.2 us)
Async XLA Ops:
  7.2 3.2 copy-start
  17.2 55.5 %all-to-all-start = ((bf16[16,2,56,1024]{3,2,1,0:T(8,128)(2,1)}), bf16[16,2,56,1024]{3,2,1,0:T(8,128)(2,1)}, u32[]{:S(2)}, u32[]{:S(2)}) async-start(bf16[16,2,56,1024]{3,2,1,0:T(8,128)(2,1)} %broadcast_select_fusion), calls=%async_computation | async-start | bytes 7340032 | tf_op jit(solution)/shard_map/all_to_all | solution.py:104
  76.6 2.7 copy-start.4
  79.2 163.4 %all-gather.2.cloned.1.call-start = ((), (), s32[]{:S(2)}) async-start(), calls=%async_computation.1 | async-start | bytes 31195136 | tf_op jit(solution)/shard_map/all_gather | solution.py:54
  81.4 1.2 copy-start.2
  84.1 193.7 %copy-start.3 = (bf16[1,112,2048]{2,1,0:T(8,128)(2,1)S(1)}, bf16[1,112,2048]{2,1,0:T(8,128)(2,1)}, u32[]{:S(2)}) copy-start(bf16[1,112,2048]{2,1,0:T(8,128)(2,1)} %param.14) | copy-start | bytes 1376260
  497.0 1.6 copy-start.1
Sparse Core Ops, SparseCore 0:
  82.8 159.7 all-gather.1
where the time goes:
time: 508 us; the launch traced here: 506 us
  waiting for transfers between devices  204 us (40%)
  local copies, waits for them, and re-layouts  127 us (25%)
  matrix products  65.1 us (13%)
  other arithmetic  49.5 us (10%)
  loops' own time  38.6 us (8%)
  between operations  14.2 us (3%)
  starting transfers between devices  6.84 us (1%)
    all_gather x1, waiting for transfers between devices, fold_attention(): piece = lax.all_gather(blended, 'seq', axis=0, tiled=True)  159 us
    slice x28, local copies, waits for them, and re-layouts, take_block(): key_part[:, KV_HEADS * HEAD_DIM:].reshape(block_rows, KV_HEADS, HEAD_DIM)  52.1 us
    all_to_all x1, waiting for transfers between devices, body(): lax.all_to_all(outgoing, 'req', split_axis=0, concat_axis=0, tiled=True)  45.7 us
    dot_general x28, matrix products, update(): jnp.einsum('qkgp,pkd->qkgd', weights.astype(jnp.bfloat16), value_rows, pr...  42.1 us
    another operation x1, loops' own time, fold_attention(): lax.scan(take_block, carry_all, jnp.arange(absorb_row_count // block_rows))  36.9 us
    while x1, local copies, waits for them, and re-layouts, fold_attention(): lax.scan(take_block, carry_all, jnp.arange(absorb_row_count // block_rows))  35.1 us
    reduce_sum x28, other arithmetic, update(): weight_sum = weight_sum * rescale + jnp.sum(weights, axis=-1)  33.8 us
    dot_general x28, matrix products, update(): jnp.einsum('qkgd,pkd->qkgp', query_split, key_rows, preferred_element_typ...  23.1 us
  transfers between devices with their start and end apart: 2, of which 2 were waited for; matrix products, arithmetic and copies ran while one was open for 1% of the time, Pallas kernels for 0%

commit v1 on v0

--- a/solution.py
+++ b/solution.py
@@ -12,6 +12,24 @@
 Q_WIDTH = 2048
 KV_WIDTH = 1024
 GROUP = 4
+
+
+def _touch_heads(packet, where_dim, mine):
+    u_next, row_out = (packet.shape[:where_dim], packet.shape[where_dim + 1 :])
+    a_now = packet.reshape(*u_next, mine, -1, *row_out)
+    oldest = jnp.moveaxis(a_now, where_dim, 0)
+    return oldest
+
+
+def _recover_corner(values, pos_dim):
+    values = jnp.moveaxis(values, 0, pos_dim)
+    everything = values.shape
+    base_arr = values.reshape(
+        *everything[:pos_dim],
+        everything[pos_dim] * everything[pos_dim + 1],
+        *everything[pos_dim + 2 :]
+    )
+    return base_arr
 
 
 def update(carry_state, query_rows, query_pos, key_rows, value_rows, key_pos):
@@ -101,7 +119,18 @@
     send_slot = jnp.sum(jnp.where(slot_hit, passage_slot[:, :, None], 0), axis=1)
     outgoing = jnp.take(store_shard, send_slot.reshape(-1), axis=0)
     outgoing = outgoing.reshape(req_count, owner_cap, PASSAGE, KV_WIDTH)
-    incoming = lax.all_to_all(outgoing, "req", split_axis=0, concat_axis=0, tiled=True)
+    z_new = lax.axis_size("req")
+    odd = lax.axis_index("req")
+    block_next, built = (z_new, odd)
+    reached = _touch_heads(outgoing, 0, block_next)
+    made = [reached[built]]
+    for to_i in range(1, block_next):
+        local_now = reached[built ^ to_i]
+        y2 = lax.ppermute(local_now, "req", [(pp, pp ^ to_i) for pp in range(block_next)])
+        made.append(y2)
+    newest = jnp.stack(made, axis=0)
+    reached = newest[built ^ jnp.arange(block_next)]
+    incoming = _recover_corner(reached, 0)
     my_rank = lax.dynamic_index_in_dim(rank_table, req_index, 0, keepdims=False)
     flat_slot = my_owner * owner_cap + my_rank
     cached = jnp.take(incoming.reshape(req_count * owner_cap, PASSAGE, KV_WIDTH), flat_slot, axis=0)

time: 508 us -> 528 us (1.039)
  starting transfers between devices: 6.84 us -> 28.2 us
  waiting for transfers between devices: 204 us -> 183 us
  local copies, waits for them, and re-layouts: 127 us -> 146 us
    all_to_all x1 -> x0, waiting for transfers between devices: 45.7 us -> none  [body(): lax.all_to_all(outgoing, 'req', split_axis=0, concat_axis=0, tiled=True)]
    ppermute x0 -> x15, waiting for transfers between devices: none -> 35.7 us  [body(): lax.ppermute(local_now, 'req', [(pp, pp ^ to_i) for pp in range(block_nex...]
    ppermute x0 -> x15, starting transfers between devices: none -> 28.2 us  [body(): lax.ppermute(local_now, 'req', [(pp, pp ^ to_i) for pp in range(block_nex...]
    all_gather x1, waiting for transfers between devices: 159 us -> 148 us  [fold_attention(): piece = lax.all_gather(blended, 'seq', axis=0, tiled=True)]
    unnamed x12 -> x28, local copies, waits for them, and re-layouts: 1.91 us -> 11.9 us
    all_to_all x1 -> x0, starting transfers between devices: 6.8 us -> none  [body(): lax.all_to_all(outgoing, 'req', split_axis=0, concat_axis=0, tiled=True)]
  transfers between devices with their start and end apart: 2 -> 16, of which waited for: 2 -> 7; matrix products, arithmetic and copies ran while one was open for 1% -> 3% of each run, Pallas kernels for 0% -> 0%
where the time goes in v1:
time: 528 us; the launch traced here: 525 us
  waiting for transfers between devices  183 us (35%)
  local copies, waits for them, and re-layouts  146 us (28%)
  matrix products  65.1 us (12%)
  other arithmetic  50.2 us (10%)
  loops' own time  38.6 us (7%)
  starting transfers between devices  28.2 us (5%)
  between operations  14.3 us (3%)
    all_gather x1, waiting for transfers between devices, fold_attention(): piece = lax.all_gather(blended, 'seq', axis=0, tiled=True)  148 us
    slice x28, local copies, waits for them, and re-layouts, take_block(): key_part[:, KV_HEADS * HEAD_DIM:].reshape(block_rows, KV_HEADS, HEAD_DIM)  52.1 us
    dot_general x28, matrix products, update(): jnp.einsum('qkgp,pkd->qkgd', weights.astype(jnp.bfloat16), value_rows, pr...  42 us
    another operation x1, loops' own time, fold_attention(): lax.scan(take_block, carry_all, jnp.arange(absorb_row_count // block_rows))  36.9 us
    ppermute x15, waiting for transfers between devices, body(): lax.ppermute(local_now, 'req', [(pp, pp ^ to_i) for pp in range(block_nex...  35.7 us
    while x1, local copies, waits for them, and re-layouts, fold_attention(): lax.scan(take_block, carry_all, jnp.arange(absorb_row_count // block_rows))  35.6 us
    reduce_sum x28, other arithmetic, update(): weight_sum = weight_sum * rescale + jnp.sum(weights, axis=-1)  33.8 us
    ppermute x15, starting transfers between devices, body(): lax.ppermute(local_now, 'req', [(pp, pp ^ to_i) for pp in range(block_nex...  28.2 us
  transfers between devices with their start and end apart: 16, of which 7 were waited for; matrix products, arithmetic and copies ran while one was open for 3% of the time, Pallas kernels for 0%

profile of v1, /device:TPU:225, one launch (start us, length us, event | category | flops | bytes accessed | tf_op | source)
XLA Modules:
  0.0 525.4 jit_solution(5510074260515025566)
XLA Ops:
  11.6 2.6 gather_fusion
  14.2 4.3 broadcast_select_fusion
  18.5 3.5 dynamic-slice_bitcast_fusion
  23.3 2.6 collective-permute-start.1
  29.5 4.8 collective-permute-start.5
  35.0 10.9 %collective-permute-done.1 = bf16[1,2,56,1024]{3,2,1,0:T(8,128)(2,1)S(1)} collective-permute-done((bf16[1,2,56,1024]{3,2,1,0:T(8,128)(2,1)}, bf16[1,2,56,1024]{3,2,1,0:T(8,128)(2,1)S(1)}, u32[]{:S(2)}, u32[]{:S(2)}) %collective-permute-start.1) | collective-permute-done | bytes 229408 | tf_op jit(solution)/shard_map/ppermute | solution.py:129
  47.5 2.5 collective-permute-start.7
  51.3 6.3 %collective-permute-start.9 = (bf16[1,2,56,1024]{3,2,1,0:T(8,128)(2,1)S(1)}, bf16[1,2,56,1024]{3,2,1,0:T(8,128)(2,1)S(1)}, u32[]{:S(2)}, u32[]{:S(2)}) collective-permute-start(bf16[1,2,56,1024]{3,2,1,0:T(8,128)(2,1)S(1)} %get-tuple-element.243), channel_id=1, source_target_pairs={{0,160},{16,176},{32,128},{48,144},{64,224},{80,240},{96,192},{112... | collective-permute-start | bytes 688136 | tf_op jit(solution)/shard_map/ppermute | solution.py:129
  62.6 5.9 %collective-permute-start.13 = (bf16[1,2,56,1024]{3,2,1,0:T(8,128)(2,1)S(1)}, bf16[1,2,56,1024]{3,2,1,0:T(8,128)(2,1)S(1)}, u32[]{:S(2)}, u32[]{:S(2)}) collective-permute-start(bf16[1,2,56,1024]{3,2,1,0:T(8,128)(2,1)S(1)} %get-tuple-element.239), channel_id=1, source_target_pairs={{0,224},{16,240},{32,192},{48,208},{64,160},{80,176},{96,128},{112... | collective-permute-start | bytes 688136 | tf_op jit(solution)/shard_map/ppermute | solution.py:129
  70.5 5.0 collective-permute-done.10
  76.2 3.6 collective-permute-done.11
  80.6 3.0 collective-permute-done.12
  84.3 4.4 collective-permute-done.13
  89.4 8.7 %collective-permute-done.14 = bf16[1,2,56,1024]{3,2,1,0:T(8,128)(2,1)S(1)} collective-permute-done((bf16[1,2,56,1024]{3,2,1,0:T(8,128)(2,1)S(1)}, bf16[1,2,56,1024]{3,2,1,0:T(8,128)(2,1)S(1)}, u32[]{:S(2)}, u32[]{:S(2)}) %collective-permute-start.14) | collective-permute-done | bytes 229408 | tf_op jit(solution)/shard_map/ppermute | solution.py:129
  98.8 4.7 gather_fusion.1
  103.5 4.1 gather_fusion.2
  110.2 2.3 scatter_custom_fusion
  115.2 147.5 %all-gather.2.cloned.1.call-done = bf16[14336,1024]{1,0:T(8,128)(2,1)} async-done(((bf16[896,1024]{1,0:T(8,128)(2,1)}), bf16[14336,1024]{1,0:T(8,128)(2,1)}) %all-gather.2.cloned.1.call-update) | async-done | bytes 29360144 | tf_op jit(solution)/shard_map/all_gather | solution.py:72
  262.7 35.6 %copy.27 = bf16[14336,1024]{0,1:T(8,128)(2,1)} copy(bf16[14336,1024]{1,0:T(8,128)(2,1)} %all-gather.2.cloned.1.call-done) | data formatting | bytes 58720256 | tf_op jit(solution)/shard_map/while | solution.py:96
  298.5 218.4 %while.15 = (s32[]{:T(128)}, f32[112,4,4]{0,2,1:T(4,128)S(1)}, f32[112,4,4]{0,2,1:T(4,128)S(1)}, f32[112,4,4,128]{3,0,2,1:T(8,128)S(1)}, s32[28]{0:T(128)S(1)}, ...) while((s32[]{:T(128)}, f32[112,4,4]{0,2,1:T(4,128)S(1)}, ...), condition=%wide.region_10.11_spmd, body=%wide.region_5.10_spmd.sunk | while | flops 482209792 | bytes 17720068 | solution.py:96
  300.4 5.9 %conditional.2 = ((f32[112,4,4]{0,2,1:T(4,128)S(1)}, f32[112,4,4]{0,2,1:T(4,128)S(1)}, f32[112,4,4,128]{3,0,2,1:T(8,128)S(1)})) conditional(s32[]{:T(128)} %convert_element_type.61, (f32[112,4,4]{0,2,1:T(4,128)S(1)}, f32[112,4,4]{0,2,1:T(4,128)S(1)}, f32[112,4,4,128]{3,0,2,1:T(8,128)S(1)}) %tuple.67, (s32[]{:T(128)}, s32[512]{0:T(512)S(1)}, ...), branch_computations={%region_6.6_spmd, %region_7.9_spmd} | conditional | flops 482209792 | bytes 17717786 | solution.py:85
  308.2 5.9 %conditional.2 = ((f32[112,4,4]{0,2,1:T(4,128)S(1)}, f32[112,4,4]{0,2,1:T(4,128)S(1)}, f32[112,4,4,128]{3,0,2,1:T(8,128)S(1)})) conditional(s32[]{:T(128)} %convert_element_type.61, (f32[112,4,4]{0,2,1:T(4,128)S(1)}, f32[112,4,4]{0,2,1:T(4,128)S(1)}, f32[112,4,4,128]{3,0,2,1:T(8,128)S(1)}) %tuple.67, (s32[]{:T(128)}, s32[512]{0:T(512)S(1)}, ...), branch_computations={%region_6.6_spmd, %region_7.9_spmd} | conditional | flops 482209792 | bytes 17717786 | solution.py:85
  316.0 5.9 %conditional.2 = ((f32[112,4,4]{0,2,1:T(4,128)S(1)}, f32[112,4,4]{0,2,1:T(4,128)S(1)}, f32[112,4,4,128]{3,0,2,1:T(8,128)S(1)})) conditional(s32[]{:T(128)} %convert_element_type.61, (f32[112,4,4]{0,2,1:T(4,128)S(1)}, f32[112,4,4]{0,2,1:T(4,128)S(1)}, f32[112,4,4,128]{3,0,2,1:T(8,128)S(1)}) %tuple.67, (s32[]{:T(128)}, s32[512]{0:T(512)S(1)}, ...), branch_computations={%region_6.6_spmd, %region_7.9_spmd} | conditional | flops 482209792 | bytes 17717786 | solution.py:85
  323.8 5.9 %conditional.2 = ((f32[112,4,4]{0,2,1:T(4,128)S(1)}, f32[112,4,4]{0,2,1:T(4,128)S(1)}, f32[112,4,4,128]{3,0,2,1:T(8,128)S(1)})) conditional(s32[]{:T(128)} %convert_element_type.61, (f32[112,4,4]{0,2,1:T(4,128)S(1)}, f32[112,4,4]{0,2,1:T(4,128)S(1)}, f32[112,4,4,128]{3,0,2,1:T(8,128)S(1)}) %tuple.67, (s32[]{:T(128)}, s32[512]{0:T(512)S(1)}, ...), branch_computations={%region_6.6_spmd, %region_7.9_spmd} | conditional | flops 482209792 | bytes 17717786 | solution.py:85
  331.6 5.9 %conditional.2 = ((f32[112,4,4]{0,2,1:T(4,128)S(1)}, f32[112,4,4]{0,2,1:T(4,128)S(1)}, f32[112,4,4,128]{3,0,2,1:T(8,128)S(1)})) conditional(s32[]{:T(128)} %convert_element_type.61, (f32[112,4,4]{0,2,1:T(4,128)S(1)}, f32[112,4,4]{0,2,1:T(4,128)S(1)}, f32[112,4,4,128]{3,0,2,1:T(8,128)S(1)}) %tuple.67, (s32[]{:T(128)}, s32[512]{0:T(512)S(1)}, ...), branch_computations={%region_6.6_spmd, %region_7.9_spmd} | conditional | flops 482209792 | bytes 17717786 | solution.py:85
  339.4 5.9 %conditional.2 = ((f32[112,4,4]{0,2,1:T(4,128)S(1)}, f32[112,4,4]{0,2,1:T(4,128)S(1)}, f32[112,4,4,128]{3,0,2,1:T(8,128)S(1)})) conditional(s32[]{:T(128)} %convert_element_type.61, (f32[112,4,4]{0,2,1:T(4,128)S(1)}, f32[112,4,4]{0,2,1:T(4,128)S(1)}, f32[112,4,4,128]{3,0,2,1:T(8,128)S(1)}) %tuple.67, (s32[]{:T(128)}, s32[512]{0:T(512)S(1)}, ...), branch_computations={%region_6.6_spmd, %region_7.9_spmd} | conditional | flops 482209792 | bytes 17717786 | solution.py:85
  347.2 5.9 %conditional.2 = ((f32[112,4,4]{0,2,1:T(4,128)S(1)}, f32[112,4,4]{0,2,1:T(4,128)S(1)}, f32[112,4,4,128]{3,0,2,1:T(8,128)S(1)})) conditional(s32[]{:T(128)} %convert_element_type.61, (f32[112,4,4]{0,2,1:T(4,128)S(1)}, f32[112,4,4]{0,2,1:T(4,128)S(1)}, f32[112,4,4,128]{3,0,2,1:T(8,128)S(1)}) %tuple.67, (s32[]{:T(128)}, s32[512]{0:T(512)S(1)}, ...), branch_computations={%region_6.6_spmd, %region_7.9_spmd} | conditional | flops 482209792 | bytes 17717786 | solution.py:85
  355.0 5.9 %conditional.2 = ((f32[112,4,4]{0,2,1:T(4,128)S(1)}, f32[112,4,4]{0,2,1:T(4,128)S(1)}, f32[112,4,4,128]{3,0,2,1:T(8,128)S(1)})) conditional(s32[]{:T(128)} %convert_element_type.61, (f32[112,4,4]{0,2,1:T(4,128)S(1)}, f32[112,4,4]{0,2,1:T(4,128)S(1)}, f32[112,4,4,128]{3,0,2,1:T(8,128)S(1)}) %tuple.67, (s32[]{:T(128)}, s32[512]{0:T(512)S(1)}, ...), branch_computations={%region_6.6_spmd, %region_7.9_spmd} | conditional | flops 482209792 | bytes 17717786 | solution.py:85
  362.8 5.9 %conditional.2 = ((f32[112,4,4]{0,2,1:T(4,128)S(1)}, f32[112,4,4]{0,2,1:T(4,128)S(1)}, f32[112,4,4,128]{3,0,2,1:T(8,128)S(1)})) conditional(s32[]{:T(128)} %convert_element_type.61, (f32[112,4,4]{0,2,1:T(4,128)S(1)}, f32[112,4,4]{0,2,1:T(4,128)S(1)}, f32[112,4,4,128]{3,0,2,1:T(8,128)S(1)}) %tuple.67, (s32[]{:T(128)}, s32[512]{0:T(512)S(1)}, ...), branch_computations={%region_6.6_spmd, %region_7.9_spmd} | conditional | flops 482209792 | bytes 17717786 | solution.py:85
  370.6 5.9 %conditional.2 = ((f32[112,4,4]{0,2,1:T(4,128)S(1)}, f32[112,4,4]{0,2,1:T(4,128)S(1)}, f32[112,4,4,128]{3,0,2,1:T(8,128)S(1)})) conditional(s32[]{:T(128)} %convert_element_type.61, (f32[112,4,4]{0,2,1:T(4,128)S(1)}, f32[112,4,4]{0,2,1:T(4,128)S(1)}, f32[112,4,4,128]{3,0,2,1:T(8,128)S(1)}) %tuple.67, (s32[]{:T(128)}, s32[512]{0:T(512)S(1)}, ...), branch_computations={%region_6.6_spmd, %region_7.9_spmd} | conditional | flops 482209792 | bytes 17717786 | solution.py:85
  378.4 5.9 %conditional.2 = ((f32[112,4,4]{0,2,1:T(4,128)S(1)}, f32[112,4,4]{0,2,1:T(4,128)S(1)}, f32[112,4,4,128]{3,0,2,1:T(8,128)S(1)})) conditional(s32[]{:T(128)} %convert_element_type.61, (f32[112,4,4]{0,2,1:T(4,128)S(1)}, f32[112,4,4]{0,2,1:T(4,128)S(1)}, f32[112,4,4,128]{3,0,2,1:T(8,128)S(1)}) %tuple.67, (s32[]{:T(128)}, s32[512]{0:T(512)S(1)}, ...), branch_computations={%region_6.6_spmd, %region_7.9_spmd} | conditional | flops 482209792 | bytes 17717786 | solution.py:85
  386.2 5.9 %conditional.2 = ((f32[112,4,4]{0,2,1:T(4,128)S(1)}, f32[112,4,4]{0,2,1:T(4,128)S(1)}, f32[112,4,4,128]{3,0,2,1:T(8,128)S(1)})) conditional(s32[]{:T(128)} %convert_element_type.61, (f32[112,4,4]{0,2,1:T(4,128)S(1)}, f32[112,4,4]{0,2,1:T(4,128)S(1)}, f32[112,4,4,128]{3,0,2,1:T(8,128)S(1)}) %tuple.67, (s32[]{:T(128)}, s32[512]{0:T(512)S(1)}, ...), branch_computations={%region_6.6_spmd, %region_7.9_spmd} | conditional | flops 482209792 | bytes 17717786 | solution.py:85
  394.0 5.9 %conditional.2 = ((f32[112,4,4]{0,2,1:T(4,128)S(1)}, f32[112,4,4]{0,2,1:T(4,128)S(1)}, f32[112,4,4,128]{3,0,2,1:T(8,128)S(1)})) conditional(s32[]{:T(128)} %convert_element_type.61, (f32[112,4,4]{0,2,1:T(4,128)S(1)}, f32[112,4,4]{0,2,1:T(4,128)S(1)}, f32[112,4,4,128]{3,0,2,1:T(8,128)S(1)}) %tuple.67, (s32[]{:T(128)}, s32[512]{0:T(512)S(1)}, ...), branch_computations={%region_6.6_spmd, %region_7.9_spmd} | conditional | flops 482209792 | bytes 17717786 | solution.py:85
  401.8 5.9 %conditional.2 = ((f32[112,4,4]{0,2,1:T(4,128)S(1)}, f32[112,4,4]{0,2,1:T(4,128)S(1)}, f32[112,4,4,128]{3,0,2,1:T(8,128)S(1)})) conditional(s32[]{:T(128)} %convert_element_type.61, (f32[112,4,4]{0,2,1:T(4,128)S(1)}, f32[112,4,4]{0,2,1:T(4,128)S(1)}, f32[112,4,4,128]{3,0,2,1:T(8,128)S(1)}) %tuple.67, (s32[]{:T(128)}, s32[512]{0:T(512)S(1)}, ...), branch_computations={%region_6.6_spmd, %region_7.9_spmd} | conditional | flops 482209792 | bytes 17717786 | solution.py:85
  409.7 5.9 %conditional.2 = ((f32[112,4,4]{0,2,1:T(4,128)S(1)}, f32[112,4,4]{0,2,1:T(4,128)S(1)}, f32[112,4,4,128]{3,0,2,1:T(8,128)S(1)})) conditional(s32[]{:T(128)} %convert_element_type.61, (f32[112,4,4]{0,2,1:T(4,128)S(1)}, f32[112,4,4]{0,2,1:T(4,128)S(1)}, f32[112,4,4,128]{3,0,2,1:T(8,128)S(1)}) %tuple.67, (s32[]{:T(128)}, s32[512]{0:T(512)S(1)}, ...), branch_computations={%region_6.6_spmd, %region_7.9_spmd} | conditional | flops 482209792 | bytes 17717786 | solution.py:85
  417.5 5.9 %conditional.2 = ((f32[112,4,4]{0,2,1:T(4,128)S(1)}, f32[112,4,4]{0,2,1:T(4,128)S(1)}, f32[112,4,4,128]{3,0,2,1:T(8,128)S(1)})) conditional(s32[]{:T(128)} %convert_element_type.61, (f32[112,4,4]{0,2,1:T(4,128)S(1)}, f32[112,4,4]{0,2,1:T(4,128)S(1)}, f32[112,4,4,128]{3,0,2,1:T(8,128)S(1)}) %tuple.67, (s32[]{:T(128)}, s32[512]{0:T(512)S(1)}, ...), branch_computations={%region_6.6_spmd, %region_7.9_spmd} | conditional | flops 482209792 | bytes 17717786 | solution.py:85
  425.3 5.9 %conditional.2 = ((f32[112,4,4]{0,2,1:T(4,128)S(1)}, f32[112,4,4]{0,2,1:T(4,128)S(1)}, f32[112,4,4,128]{3,0,2,1:T(8,128)S(1)})) conditional(s32[]{:T(128)} %convert_element_type.61, (f32[112,4,4]{0,2,1:T(4,128)S(1)}, f32[112,4,4]{0,2,1:T(4,128)S(1)}, f32[112,4,4,128]{3,0,2,1:T(8,128)S(1)}) %tuple.67, (s32[]{:T(128)}, s32[512]{0:T(512)S(1)}, ...), branch_computations={%region_6.6_spmd, %region_7.9_spmd} | conditional | flops 482209792 | bytes 17717786 | solution.py:85
  433.1 5.9 %conditional.2 = ((f32[112,4,4]{0,2,1:T(4,128)S(1)}, f32[112,4,4]{0,2,1:T(4,128)S(1)}, f32[112,4,4,128]{3,0,2,1:T(8,128)S(1)})) conditional(s32[]{:T(128)} %convert_element_type.61, (f32[112,4,4]{0,2,1:T(4,128)S(1)}, f32[112,4,4]{0,2,1:T(4,128)S(1)}, f32[112,4,4,128]{3,0,2,1:T(8,128)S(1)}) %tuple.67, (s32[]{:T(128)}, s32[512]{0:T(512)S(1)}, ...), branch_computations={%region_6.6_spmd, %region_7.9_spmd} | conditional | flops 482209792 | bytes 17717786 | solution.py:85
  440.9 5.9 %conditional.2 = ((f32[112,4,4]{0,2,1:T(4,128)S(1)}, f32[112,4,4]{0,2,1:T(4,128)S(1)}, f32[112,4,4,128]{3,0,2,1:T(8,128)S(1)})) conditional(s32[]{:T(128)} %convert_element_type.61, (f32[112,4,4]{0,2,1:T(4,128)S(1)}, f32[112,4,4]{0,2,1:T(4,128)S(1)}, f32[112,4,4,128]{3,0,2,1:T(8,128)S(1)}) %tuple.67, (s32[]{:T(128)}, s32[512]{0:T(512)S(1)}, ...), branch_computations={%region_6.6_spmd, %region_7.9_spmd} | conditional | flops 482209792 | bytes 17717786 | solution.py:85
  448.7 5.9 %conditional.2 = ((f32[112,4,4]{0,2,1:T(4,128)S(1)}, f32[112,4,4]{0,2,1:T(4,128)S(1)}, f32[112,4,4,128]{3,0,2,1:T(8,128)S(1)})) conditional(s32[]{:T(128)} %convert_element_type.61, (f32[112,4,4]{0,2,1:T(4,128)S(1)}, f32[112,4,4]{0,2,1:T(4,128)S(1)}, f32[112,4,4,128]{3,0,2,1:T(8,128)S(1)}) %tuple.67, (s32[]{:T(128)}, s32[512]{0:T(512)S(1)}, ...), branch_computations={%region_6.6_spmd, %region_7.9_spmd} | conditional | flops 482209792 | bytes 17717786 | solution.py:85
  456.5 5.9 %conditional.2 = ((f32[112,4,4]{0,2,1:T(4,128)S(1)}, f32[112,4,4]{0,2,1:T(4,128)S(1)}, f32[112,4,4,128]{3,0,2,1:T(8,128)S(1)})) conditional(s32[]{:T(128)} %convert_element_type.61, (f32[112,4,4]{0,2,1:T(4,128)S(1)}, f32[112,4,4]{0,2,1:T(4,128)S(1)}, f32[112,4,4,128]{3,0,2,1:T(8,128)S(1)}) %tuple.67, (s32[]{:T(128)}, s32[512]{0:T(512)S(1)}, ...), branch_computations={%region_6.6_spmd, %region_7.9_spmd} | conditional | flops 482209792 | bytes 17717786 | solution.py:85
  464.3 5.9 %conditional.2 = ((f32[112,4,4]{0,2,1:T(4,128)S(1)}, f32[112,4,4]{0,2,1:T(4,128)S(1)}, f32[112,4,4,128]{3,0,2,1:T(8,128)S(1)})) conditional(s32[]{:T(128)} %convert_element_type.61, (f32[112,4,4]{0,2,1:T(4,128)S(1)}, f32[112,4,4]{0,2,1:T(4,128)S(1)}, f32[112,4,4,128]{3,0,2,1:T(8,128)S(1)}) %tuple.67, (s32[]{:T(128)}, s32[512]{0:T(512)S(1)}, ...), branch_computations={%region_6.6_spmd, %region_7.9_spmd} | conditional | flops 482209792 | bytes 17717786 | solution.py:85
  472.1 5.9 %conditional.2 = ((f32[112,4,4]{0,2,1:T(4,128)S(1)}, f32[112,4,4]{0,2,1:T(4,128)S(1)}, f32[112,4,4,128]{3,0,2,1:T(8,128)S(1)})) conditional(s32[]{:T(128)} %convert_element_type.61, (f32[112,4,4]{0,2,1:T(4,128)S(1)}, f32[112,4,4]{0,2,1:T(4,128)S(1)}, f32[112,4,4,128]{3,0,2,1:T(8,128)S(1)}) %tuple.67, (s32[]{:T(128)}, s32[512]{0:T(512)S(1)}, ...), branch_computations={%region_6.6_spmd, %region_7.9_spmd} | conditional | flops 482209792 | bytes 17717786 | solution.py:85
  479.9 5.9 %conditional.2 = ((f32[112,4,4]{0,2,1:T(4,128)S(1)}, f32[112,4,4]{0,2,1:T(4,128)S(1)}, f32[112,4,4,128]{3,0,2,1:T(8,128)S(1)})) conditional(s32[]{:T(128)} %convert_element_type.61, (f32[112,4,4]{0,2,1:T(4,128)S(1)}, f32[112,4,4]{0,2,1:T(4,128)S(1)}, f32[112,4,4,128]{3,0,2,1:T(8,128)S(1)}) %tuple.67, (s32[]{:T(128)}, s32[512]{0:T(512)S(1)}, ...), branch_computations={%region_6.6_spmd, %region_7.9_spmd} | conditional | flops 482209792 | bytes 17717786 | solution.py:85
  487.7 5.9 %conditional.2 = ((f32[112,4,4]{0,2,1:T(4,128)S(1)}, f32[112,4,4]{0,2,1:T(4,128)S(1)}, f32[112,4,4,128]{3,0,2,1:T(8,128)S(1)})) conditional(s32[]{:T(128)} %convert_element_type.61, (f32[112,4,4]{0,2,1:T(4,128)S(1)}, f32[112,4,4]{0,2,1:T(4,128)S(1)}, f32[112,4,4,128]{3,0,2,1:T(8,128)S(1)}) %tuple.67, (s32[]{:T(128)}, s32[512]{0:T(512)S(1)}, ...), branch_computations={%region_6.6_spmd, %region_7.9_spmd} | conditional | flops 482209792 | bytes 17717786 | solution.py:85
  495.5 5.9 %conditional.2 = ((f32[112,4,4]{0,2,1:T(4,128)S(1)}, f32[112,4,4]{0,2,1:T(4,128)S(1)}, f32[112,4,4,128]{3,0,2,1:T(8,128)S(1)})) conditional(s32[]{:T(128)} %convert_element_type.61, (f32[112,4,4]{0,2,1:T(4,128)S(1)}, f32[112,4,4]{0,2,1:T(4,128)S(1)}, f32[112,4,4,128]{3,0,2,1:T(8,128)S(1)}) %tuple.67, (s32[]{:T(128)}, s32[512]{0:T(512)S(1)}, ...), branch_computations={%region_6.6_spmd, %region_7.9_spmd} | conditional | flops 482209792 | bytes 17717786 | solution.py:85
  503.3 5.9 %conditional.2 = ((f32[112,4,4]{0,2,1:T(4,128)S(1)}, f32[112,4,4]{0,2,1:T(4,128)S(1)}, f32[112,4,4,128]{3,0,2,1:T(8,128)S(1)})) conditional(s32[]{:T(128)} %convert_element_type.61, (f32[112,4,4]{0,2,1:T(4,128)S(1)}, f32[112,4,4]{0,2,1:T(4,128)S(1)}, f32[112,4,4,128]{3,0,2,1:T(8,128)S(1)}) %tuple.67, (s32[]{:T(128)}, s32[512]{0:T(512)S(1)}, ...), branch_computations={%region_6.6_spmd, %region_7.9_spmd} | conditional | flops 482209792 | bytes 17717786 | solution.py:85
  511.1 5.8 %conditional.2 = ((f32[112,4,4]{0,2,1:T(4,128)S(1)}, f32[112,4,4]{0,2,1:T(4,128)S(1)}, f32[112,4,4,128]{3,0,2,1:T(8,128)S(1)})) conditional(s32[]{:T(128)} %convert_element_type.61, (f32[112,4,4]{0,2,1:T(4,128)S(1)}, f32[112,4,4]{0,2,1:T(4,128)S(1)}, f32[112,4,4,128]{3,0,2,1:T(8,128)S(1)}) %tuple.67, (s32[]{:T(128)}, s32[512]{0:T(512)S(1)}, ...), branch_computations={%region_6.6_spmd, %region_7.9_spmd} | conditional | flops 482209792 | bytes 17717786 | solution.py:85
  (418 shorter events, 210.1 us)
Async XLA Ops:
  7.2 4.4 copy-start
  9.2 5.0 copy-start.5
  22.0 7.5 %collective-permute-start = (bf16[1,2,56,1024]{3,2,1,0:T(8,128)(2,1)}, bf16[1,2,56,1024]{3,2,1,0:T(8,128)(2,1)S(1)}, u32[]{:S(2)}, u32[]{:S(2)}) collective-permute-start(bf16[1,2,56,1024]{3,2,1,0:T(8,128)(2,1)} %get-tuple-element.252), channel_id=1, source_target_pairs={{0,16},{16,0},{32,48},{48,32},{64,80},{80,64},{96,112},{112,96},{1... | collective-permute-start | bytes 688136 | tf_op jit(solution)/shard_map/ppermute | solution.py:129
  23.3 22.6 %collective-permute-start.1 = (bf16[1,2,56,1024]{3,2,1,0:T(8,128)(2,1)}, bf16[1,2,56,1024]{3,2,1,0:T(8,128)(2,1)S(1)}, u32[]{:S(2)}, u32[]{:S(2)}) collective-permute-start(bf16[1,2,56,1024]{3,2,1,0:T(8,128)(2,1)} %get-tuple-element.251), channel_id=1, source_target_pairs={{0,32},{16,48},{32,0},{48,16},{64,96},{80,112},{96,64},{112,80},{1... | collective-permute-start | bytes 688136 | tf_op jit(solution)/shard_map/ppermute | solution.py:129
  25.9 21.6 %collective-permute-start.2 = (bf16[1,2,56,1024]{3,2,1,0:T(8,128)(2,1)}, bf16[1,2,56,1024]{3,2,1,0:T(8,128)(2,1)S(1)}, u32[]{:S(2)}, u32[]{:S(2)}) collective-permute-start(bf16[1,2,56,1024]{3,2,1,0:T(8,128)(2,1)} %get-tuple-element.250), channel_id=1, source_target_pairs={{0,48},{16,32},{32,16},{48,0},{64,112},{80,96},{96,80},{112,64},{1... | collective-permute-start | bytes 688136 | tf_op jit(solution)/shard_map/ppermute | solution.py:129
  25.9 24.7 %collective-permute-start.3 = (bf16[1,2,56,1024]{3,2,1,0:T(8,128)(2,1)}, bf16[1,2,56,1024]{3,2,1,0:T(8,128)(2,1)S(1)}, u32[]{:S(2)}, u32[]{:S(2)}) collective-permute-start(bf16[1,2,56,1024]{3,2,1,0:T(8,128)(2,1)} %get-tuple-element.249), channel_id=1, source_target_pairs={{0,64},{16,80},{32,96},{48,112},{64,0},{80,16},{96,32},{112,48},{1... | collective-permute-start | bytes 688136 | tf_op jit(solution)/shard_map/ppermute | solution.py:129
  27.1 24.2 %collective-permute-start.4 = (bf16[1,2,56,1024]{3,2,1,0:T(8,128)(2,1)}, bf16[1,2,56,1024]{3,2,1,0:T(8,128)(2,1)S(1)}, u32[]{:S(2)}, u32[]{:S(2)}) collective-permute-start(bf16[1,2,56,1024]{3,2,1,0:T(8,128)(2,1)} %get-tuple-element.248), channel_id=1, source_target_pairs={{0,80},{16,64},{32,112},{48,96},{64,16},{80,0},{96,48},{112,32},{1... | collective-permute-start | bytes 688136 | tf_op jit(solution)/shard_map/ppermute | solution.py:129
  29.5 28.9 %collective-permute-start.5 = (bf16[1,2,56,1024]{3,2,1,0:T(8,128)(2,1)S(1)}, bf16[1,2,56,1024]{3,2,1,0:T(8,128)(2,1)S(1)}, u32[]{:S(2)}, u32[]{:S(2)}) collective-permute-start(bf16[1,2,56,1024]{3,2,1,0:T(8,128)(2,1)S(1)} %get-tuple-element.247), channel_id=1, source_target_pairs={{0,96},{16,112},{32,64},{48,80},{64,32},{80,48},{96,0},{112,16},{1... | collective-permute-start | bytes 688136 | tf_op jit(solution)/shard_map/ppermute | solution.py:129
  45.9 13.4 %collective-permute-start.6 = (bf16[1,2,56,1024]{3,2,1,0:T(8,128)(2,1)S(1)}, bf16[1,2,56,1024]{3,2,1,0:T(8,128)(2,1)S(1)}, u32[]{:S(2)}, u32[]{:S(2)}) collective-permute-start(bf16[1,2,56,1024]{3,2,1,0:T(8,128)(2,1)S(1)} %get-tuple-element.246), channel_id=1, source_target_pairs={{0,112},{16,96},{32,80},{48,64},{64,48},{80,32},{96,16},{112,0},{1... | collective-permute-start | bytes 688136 | tf_op jit(solution)/shard_map/ppermute | solution.py:129
  47.5 14.4 %collective-permute-start.7 = (bf16[1,2,56,1024]{3,2,1,0:T(8,128)(2,1)S(1)}, bf16[1,2,56,1024]{3,2,1,0:T(8,128)(2,1)S(1)}, u32[]{:S(2)}, u32[]{:S(2)}) collective-permute-start(bf16[1,2,56,1024]{3,2,1,0:T(8,128)(2,1)S(1)} %get-tuple-element.245), channel_id=1, source_target_pairs={{0,128},{16,144},{32,160},{48,176},{64,192},{80,208},{96,224},{112... | collective-permute-start | bytes 688136 | tf_op jit(solution)/shard_map/ppermute | solution.py:129
  50.6 12.0 %collective-permute-start.8 = (bf16[1,2,56,1024]{3,2,1,0:T(8,128)(2,1)S(1)}, bf16[1,2,56,1024]{3,2,1,0:T(8,128)(2,1)S(1)}, u32[]{:S(2)}, u32[]{:S(2)}) collective-permute-start(bf16[1,2,56,1024]{3,2,1,0:T(8,128)(2,1)S(1)} %get-tuple-element.244), channel_id=1, source_target_pairs={{0,144},{16,128},{32,176},{48,160},{64,208},{80,192},{96,240},{112... | collective-permute-start | bytes 688136 | tf_op jit(solution)/shard_map/ppermute | solution.py:129
  51.3 17.9 %collective-permute-start.9 = (bf16[1,2,56,1024]{3,2,1,0:T(8,128)(2,1)S(1)}, bf16[1,2,56,1024]{3,2,1,0:T(8,128)(2,1)S(1)}, u32[]{:S(2)}, u32[]{:S(2)}) collective-permute-start(bf16[1,2,56,1024]{3,2,1,0:T(8,128)(2,1)S(1)} %get-tuple-element.243), channel_id=1, source_target_pairs={{0,160},{16,176},{32,128},{48,144},{64,224},{80,240},{96,192},{112... | collective-permute-start | bytes 688136 | tf_op jit(solution)/shard_map/ppermute | solution.py:129
  58.4 17.1 %collective-permute-start.10 = (bf16[1,2,56,1024]{3,2,1,0:T(8,128)(2,1)S(1)}, bf16[1,2,56,1024]{3,2,1,0:T(8,128)(2,1)S(1)}, u32[]{:S(2)}, u32[]{:S(2)}) collective-permute-start(bf16[1,2,56,1024]{3,2,1,0:T(8,128)(2,1)S(1)} %get-tuple-element.242), channel_id=1, source_target_pairs={{0,176},{16,160},{32,144},{48,128},{64,240},{80,224},{96,208},{112... | collective-permute-start | bytes 688136 | tf_op jit(solution)/shard_map/ppermute | solution.py:129
  59.3 20.6 %collective-permute-start.11 = (bf16[1,2,56,1024]{3,2,1,0:T(8,128)(2,1)S(1)}, bf16[1,2,56,1024]{3,2,1,0:T(8,128)(2,1)S(1)}, u32[]{:S(2)}, u32[]{:S(2)}) collective-permute-start(bf16[1,2,56,1024]{3,2,1,0:T(8,128)(2,1)S(1)} %get-tuple-element.241), channel_id=1, source_target_pairs={{0,192},{16,208},{32,224},{48,240},{64,128},{80,144},{96,160},{112... | collective-permute-start | bytes 688136 | tf_op jit(solution)/shard_map/ppermute | solution.py:129
  61.8 21.8 %collective-permute-start.12 = (bf16[1,2,56,1024]{3,2,1,0:T(8,128)(2,1)S(1)}, bf16[1,2,56,1024]{3,2,1,0:T(8,128)(2,1)S(1)}, u32[]{:S(2)}, u32[]{:S(2)}) collective-permute-start(bf16[1,2,56,1024]{3,2,1,0:T(8,128)(2,1)S(1)} %get-tuple-element.240), channel_id=1, source_target_pairs={{0,208},{16,192},{32,240},{48,224},{64,144},{80,128},{96,176},{112... | collective-permute-start | bytes 688136 | tf_op jit(solution)/shard_map/ppermute | solution.py:129
  62.6 26.0 %collective-permute-start.13 = (bf16[1,2,56,1024]{3,2,1,0:T(8,128)(2,1)S(1)}, bf16[1,2,56,1024]{3,2,1,0:T(8,128)(2,1)S(1)}, u32[]{:S(2)}, u32[]{:S(2)}) collective-permute-start(bf16[1,2,56,1024]{3,2,1,0:T(8,128)(2,1)S(1)} %get-tuple-element.239), channel_id=1, source_target_pairs={{0,224},{16,240},{32,192},{48,208},{64,160},{80,176},{96,128},{112... | collective-permute-start | bytes 688136 | tf_op jit(solution)/shard_map/ppermute | solution.py:129
  69.3 28.8 %collective-permute-start.14 = (bf16[1,2,56,1024]{3,2,1,0:T(8,128)(2,1)S(1)}, bf16[1,2,56,1024]{3,2,1,0:T(8,128)(2,1)S(1)}, u32[]{:S(2)}, u32[]{:S(2)}) collective-permute-start(bf16[1,2,56,1024]{3,2,1,0:T(8,128)(2,1)S(1)} %get-tuple-element.238), channel_id=1, source_target_pairs={{0,240},{16,224},{32,208},{48,192},{64,176},{80,160},{96,144},{112... | collective-permute-start | bytes 688136 | tf_op jit(solution)/shard_map/ppermute | solution.py:129
  107.5 2.7 copy-start.4
  110.2 152.6 %all-gather.2.cloned.1.call-start = ((), (), s32[]{:S(2)}) async-start(), calls=%async_computation | async-start | bytes 31195136 | tf_op jit(solution)/shard_map/all_gather | solution.py:72
  112.5 1.2 copy-start.2
  115.2 183.3 %copy-start.3 = (bf16[1,112,2048]{2,1,0:T(8,128)(2,1)S(1)}, bf16[1,112,2048]{2,1,0:T(8,128)(2,1)}, u32[]{:S(2)}) copy-start(bf16[1,112,2048]{2,1,0:T(8,128)(2,1)} %param.14) | copy-start | bytes 1376260
  516.9 1.6 copy-start.1
Sparse Core Ops, SparseCore 0:
  113.9 148.7 all-gather.1
